TPU v7x, 32 devices: a whole 2x2x4 slice. The times are simulated.
32 devices in a mesh: row: 8 (over y, x, core), col: 4 (over z).
Axes of the slice: x: 2, y: 2, z: 4, core: 2. Of those that a mesh axis runs over, the one named last changes fastest.
Arguments:
- tensor: float32 [128, 128, 768], P('row', 'col'), may hold values from -6 to 6
- start_one: float32 [128, 64], P('row'), may hold values from -0.5 to 0.5
- start_two: float32 [128, 64], P('col'), may hold values from -0.5 to 0.5
- start_three: float32 [768, 64], replicated, may hold values from -0.21875 to 0.21875
Outputs:
- factor_one: float32 [128, 64], replicated
- factor_two: float32 [128, 64], replicated
- factor_three: float32 [768, 64], replicated
- core: float32 [64, 64, 64], P(None, 'row', 'col')
All inputs are finite; a program needn't handle non-finite values.
Results may differ from a plain program's by a relative error of at most 0.0003.
Values sent between devices are 32-bit elements; how exact they have to be, the bound alone decides.
A program may use at most 64 MiB of HBM per device.

v0:
```python
import math

import jax
import jax.numpy as jnp
from jax import lax
from jax.sharding import PartitionSpec as P

STEPS = 4


HIGHEST = lax.Precision.HIGHEST


def product(left, right):
    return jnp.dot(left, right, precision=HIGHEST, preferred_element_type=jnp.float32)


def left_product(left, right):
    return lax.dot_general(
        left, right, (((0,), (0,)), ((), ())), precision=HIGHEST, preferred_element_type=jnp.float32
    )


def right_product(left, right):
    return lax.dot_general(
        left, right, (((1,), (1,)), ((), ())), precision=HIGHEST, preferred_element_type=jnp.float32
    )


def cross_product(left, right):
    return lax.dot_general(
        left, right, (((0,), (1,)), ((), ())), precision=HIGHEST, preferred_element_type=jnp.float32
    )


def orthonormal(matrix, inner):
    lower = jnp.linalg.cholesky(inner)
    return jax.scipy.linalg.solve_triangular(lower, matrix.T, lower=True).T


def pairing(local, block_rows):
    return right_product(local, block_rows)


def settle(gram_whole, basis):
    for iteration in range(STEPS):
        image = product(gram_whole, basis)
        basis = orthonormal(image, left_product(image, image))
    return basis


def on_device(tensor, start_one, start_two, start_three):
    rows_one, rows_two, depth = tensor.shape
    rank = start_three.shape[1]
    flat = tensor.reshape(rows_one * rows_two, depth)
    contracted = cross_product(start_three, flat).reshape(rank, rows_one, rows_two)
    part_one = jnp.einsum("cij,jb->ibc", contracted, start_two, precision=HIGHEST).reshape(
        rows_one, rank * rank
    )
    slab_one = lax.psum_scatter(part_one, "col", scatter_dimension=1, tiled=True)
    slab_rows_one = lax.all_gather(slab_one, "row", axis=0, tiled=True)
    gram_one = lax.psum(right_product(slab_rows_one, slab_rows_one), "col")
    basis_one = settle(gram_one, lax.all_gather(start_one, "row", axis=0, tiled=True))
    own_one = lax.dynamic_slice_in_dim(basis_one, lax.axis_index("row") * rows_one, rows_one, 0)
    part_two = jnp.einsum("cij,ia->jac", contracted, own_one, precision=HIGHEST).reshape(
        rows_two, rank * rank
    )
    slab_two = lax.psum_scatter(part_two, "row", scatter_dimension=1, tiled=True)
    slab_rows_two = lax.all_gather(slab_two, "col", axis=0, tiled=True)
    gram_two = lax.psum(right_product(slab_rows_two, slab_rows_two), "row")
    basis_two = settle(gram_two, lax.all_gather(start_two, "col", axis=0, tiled=True))
    own_two = lax.dynamic_slice_in_dim(basis_two, lax.axis_index("col") * rows_two, rows_two, 0)
    received = lax.all_to_all(tensor, "row", split_axis=2, concat_axis=0, tiled=True)
    count, items, cells = received.shape
    merged = left_product(basis_one, received.reshape(count, items * cells))
    mixed = merged.reshape(rank, items, cells)
    part_three = jnp.einsum("ajk,jb->kba", mixed, own_two, precision=HIGHEST)
    cells_here = part_three.shape[0]
    slab_three = lax.psum_scatter(
        part_three.reshape(cells_here, rank * rank), "col", scatter_dimension=1, tiled=True
    )
    gram_part_three = pairing(slab_three, lax.all_gather(slab_three, "row", axis=0, tiled=True))
    gram_three = lax.psum(gram_part_three, "col")
    basis_three = start_three
    own_three = start_three
    for iteration in range(STEPS):
        image = product(gram_three, basis_three)
        inner = lax.psum(left_product(image, image), "row")
        own_three = orthonormal(image, inner)
        basis_three = lax.all_gather(own_three, "row", axis=0, tiled=True)
    core_part = left_product(own_three, slab_three)
    core_part = core_part.reshape(rank, core_part.shape[1] // rank, rank)
    core = lax.psum_scatter(core_part, "row", scatter_dimension=2, tiled=True).transpose(0, 2, 1)
    factor_one = basis_one * math.sqrt(basis_one.shape[0])
    factor_two = basis_two * math.sqrt(basis_two.shape[0])
    factor_three = basis_three * math.sqrt(basis_three.shape[0])
    return (factor_one, factor_two, factor_three, core)


def solution(mesh):
    return jax.shard_map(
        on_device,
        mesh=mesh,
        in_specs=(P("row", "col", None), P("row", None), P("col", None), P()),
        out_specs=(P(), P(), P(), P(None, "row", "col")),
        check_vma=False,
    )
```

profile of v0, /device:TPU:0, one launch (start us, length us, event | category | flops | bytes accessed | tf_op | source)
XLA Modules:
  0.0 638.1 jit_solution(973068163309146630)
XLA Ops:
  13.1 22.8 %reduce-scatter.5.cloned.1.call-done = f32[16,1024]{1,0:T(8,128)} async-done(((f32[16,4096]{1,0:T(8,128)}), f32[16,1024]{1,0:T(8,128)}) %reduce-scatter.5.cloned.1.call-update) | async-done | bytes 65552 | tf_op jit(solution)/shard_map/reduce_scatter | solution.py:60
  35.9 10.1 %all_gather.27 = f32[128,1024]{1,0:T(8,128)S(1)} all-gather(f32[16,1024]{1,0:T(8,128)} %reduce-scatter.5.cloned.1.call-done), channel_id=1, replica_groups=mesh['row'=8,'col'=4] {'row'}, dimensions={0}, use_global_device_ids=true | all-gather | bytes 589824 | tf_op jit(solution)/shard_map/all_gather | solution.py:61
  52.3 7.6 %reshape.61 = f32[8,1,49152]{2,1,0:T(1,128)} reshape(f32[768,16,32]{2,1,0:T(8,128)} %bitcast.262) | data formatting | bytes 3145728
  63.7 24.3 %all_gather.28 = f32[128,64]{1,0:T(8,128)S(1)} all-gather(f32[16,64]{1,0:T(8,128)S(1)} %copy-done.7), channel_id=1, replica_groups=mesh['row'=8,'col'=4] {'row'}, dimensions={0}, use_global_device_ids=true | all-gather | bytes 36864 | tf_op jit(solution)/shard_map/all_gather | solution.py:63
  89.5 5.8 cholesky.194
  103.2 5.8 cholesky.205
  116.9 5.8 cholesky.216
  129.8 5.8 cholesky.227
  144.4 13.1 %all_gather.30 = f32[128,64]{1,0:T(8,128)S(1)} all-gather(f32[32,64]{1,0:T(8,128)S(1)} %copy-done.6), channel_id=1, replica_groups=mesh['row'=8,'col'=4] {'col'}, dimensions={0}, use_global_device_ids=true | all-gather | bytes 40960 | tf_op jit(solution)/shard_map/all_gather | solution.py:71
  157.6 18.4 %reduce-scatter.7.cloned.1.call-done = f32[32,512]{1,0:T(8,128)} async-done(((f32[32,4096]{1,0:T(8,128)}), f32[32,512]{1,0:T(8,128)}) %reduce-scatter.7.cloned.1.call-update) | async-done | bytes 65552 | tf_op jit(solution)/shard_map/reduce_scatter | solution.py:68
  176.0 14.0 %all_gather.29 = f32[128,512]{1,0:T(8,128)S(1)} all-gather(f32[32,512]{1,0:T(8,128)} %reduce-scatter.7.cloned.1.call-done), channel_id=1, replica_groups=mesh['row'=8,'col'=4] {'col'}, dimensions={0}, use_global_device_ids=true | all-gather | bytes 327680 | tf_op jit(solution)/shard_map/all_gather | solution.py:69
  213.9 31.0 %all-reduce.6.cloned.1.call-done = f32[128,128]{1,0:T(8,128)} async-done(((f32[128,128]{1,0:T(8,128)}), f32[128,128]{1,0:T(8,128)}) %all-reduce.6.cloned.1.call-update) | async-done | bytes 65552 | tf_op jit(solution)/shard_map/psum | solution.py:70
  246.4 5.8 cholesky.238
  260.1 5.8 cholesky.249
  273.9 5.8 cholesky.260
  286.7 5.8 cholesky.271
  304.2 43.1 %reduce-scatter.9.cloned.1.call-done = f32[96,1024]{0,1:T(8,128)} async-done(((f32[96,4096]{0,1:T(8,128)}), f32[96,1024]{0,1:T(8,128)}) %reduce-scatter.9.cloned.1.call-update) | async-done | bytes 393232 | tf_op jit(solution)/shard_map/reduce_scatter | solution.py:79
  349.4 31.5 %all-gather.6.cloned.1.call-done = f32[768,1024]{1,0:T(8,128)} async-done(((f32[96,1024]{1,0:T(8,128)}), f32[768,1024]{1,0:T(8,128)}) %all-gather.6.cloned.1.call-update) | async-done | bytes 3145744 | tf_op jit(solution)/shard_map/all_gather | solution.py:82
  386.9 35.4 %all-reduce.8.cloned.1.call-done = f32[96,768]{1,0:T(8,128)} async-done(((f32[96,768]{1,0:T(8,128)}), f32[96,768]{1,0:T(8,128)}) %all-reduce.8.cloned.1.call-update) | async-done | bytes 294928 | tf_op jit(solution)/shard_map/psum | solution.py:83
  424.0 22.4 %psum.52 = f32[64,64]{0,1:T(8,128)S(1)} all-reduce(f32[64,64]{0,1:T(8,128)S(1)} %fusion.96), channel_id=1, replica_groups=mesh['row'=8,'col'=4] {'row'}, use_global_device_ids=true, to_apply=%region_8.11 | all-reduce | flops 4096 | bytes 32768 | tf_op jit(solution)/shard_map/psum | solution.py:88
  446.4 5.8 cholesky.282
  458.8 9.3 %all-gather = f32[8,96,64]{1,2,0:T(8,128)S(1)} all-gather(f32[1,96,64]{1,2,0:T(8,128)S(1)} %convolution_bitcast_fusion.5), channel_id=1, replica_groups=mesh['row'=8,'col'=4] {'row'}, dimensions={0}, use_global_device_ids=true | all-gather | bytes 221184 | tf_op jit(solution)/shard_map/all_gather | solution.py:90
  469.0 23.9 %psum.53 = f32[64,64]{0,1:T(8,128)S(1)} all-reduce(f32[64,64]{0,1:T(8,128)S(1)} %fusion.98), channel_id=1, replica_groups=mesh['row'=8,'col'=4] {'row'}, use_global_device_ids=true, to_apply=%region_9.0 | all-reduce | flops 4096 | bytes 32768 | tf_op jit(solution)/shard_map/psum | solution.py:88
  493.0 5.8 cholesky.293
  505.3 8.3 %all-gather.1 = f32[8,96,64]{1,2,0:T(8,128)S(1)} all-gather(f32[1,96,64]{1,2,0:T(8,128)S(1)} %convolution_bitcast_fusion.4), channel_id=1, replica_groups=mesh['row'=8,'col'=4] {'row'}, dimensions={0}, use_global_device_ids=true | all-gather | bytes 221184 | tf_op jit(solution)/shard_map/all_gather | solution.py:90
  514.6 23.6 %psum.54 = f32[64,64]{0,1:T(8,128)S(1)} all-reduce(f32[64,64]{0,1:T(8,128)S(1)} %fusion.100), channel_id=1, replica_groups=mesh['row'=8,'col'=4] {'row'}, use_global_device_ids=true, to_apply=%region_10.0 | all-reduce | flops 4096 | bytes 32768 | tf_op jit(solution)/shard_map/psum | solution.py:88
  538.3 5.8 cholesky.304
  550.6 9.3 %all-gather.2 = f32[8,96,64]{1,2,0:T(8,128)S(1)} all-gather(f32[1,96,64]{1,2,0:T(8,128)S(1)} %convolution_bitcast_fusion.3), channel_id=1, replica_groups=mesh['row'=8,'col'=4] {'row'}, dimensions={0}, use_global_device_ids=true | all-gather | bytes 221184 | tf_op jit(solution)/shard_map/all_gather | solution.py:90
  560.8 23.6 %psum.55 = f32[64,64]{0,1:T(8,128)S(1)} all-reduce(f32[64,64]{0,1:T(8,128)S(1)} %fusion.102), channel_id=1, replica_groups=mesh['row'=8,'col'=4] {'row'}, use_global_device_ids=true, to_apply=%region_11.15 | all-reduce | flops 4096 | bytes 32768 | tf_op jit(solution)/shard_map/psum | solution.py:88
  584.5 5.8 cholesky.315
  599.4 8.3 %all-gather.3 = f32[8,96,64]{1,2,0:T(8,128)S(1)} all-gather(f32[1,96,64]{1,2,0:T(8,128)S(1)} %bitcast.267), channel_id=1, replica_groups=mesh['row'=8,'col'=4] {'row'}, dimensions={0}, use_global_device_ids=true | all-gather | bytes 221184 | tf_op jit(solution)/shard_map/all_gather | solution.py:90
  608.7 22.2 %reduce-scatter.11.cloned.1.call-done = f32[64,16,8]{0,1,2:T(8,128)} async-done(((f32[64,16,64]{0,1,2:T(8,128)}), f32[64,16,8]{0,1,2:T(8,128)}) %reduce-scatter.11.cloned.1.call-update) | async-done | bytes 32784 | tf_op jit(solution)/shard_map/reduce_scatter | solution.py:93
  (177 shorter events, 150.3 us)
Async XLA Ops:
  7.2 0.9 copy-start
  7.2 3.7 copy-start.6
  7.2 28.7 %reduce-scatter.5.cloned.1.call-start = ((), (), s32[]{:S(2)}) async-start(), calls=%async_computation.5 | async-start | bytes 327680 | tf_op jit(solution)/shard_map/reduce_scatter | solution.py:60
  12.1 35.1 %copy-start.1 = (f32[16,32,768]{2,1,0:T(8,128)S(1)}, f32[16,32,768]{2,1,0:T(8,128)}, u32[]{:S(2)}) copy-start(f32[16,32,768]{2,1,0:T(8,128)} %param.9) | copy-start | bytes 4718596
  13.0 75.0 %all-reduce.4.cloned.1.call-start = ((), (), s32[]{:S(2)}) async-start(), calls=%async_computation.6 | async-start | bytes 131072 | tf_op jit(solution)/shard_map/psum | solution.py:62
  59.9 3.8 copy-start.7
  59.9 131.4 %all-to-all-start = ((f32[8,1,49152]{2,1,0:T(1,128)}), f32[8,1,49152]{2,1,0:T(1,128)S(1)}, u32[]{:S(2)}, u32[]{:S(2)}) async-start(f32[8,1,49152]{2,1,0:T(1,128)} %reshape.61), calls=%async_computation.2 | async-start | bytes 3145728 | tf_op jit(solution)/shard_map/all_to_all | solution.py:73
  63.6 112.3 %reduce-scatter.7.cloned.1.call-start = ((), (), s32[]{:S(2)}) async-start(), calls=%async_computation.7 | async-start | bytes 589824 | tf_op jit(solution)/shard_map/reduce_scatter | solution.py:68
  88.0 41.2 %copy-start.4 = (f32[128,128]{1,0:T(8,128)S(1)}, f32[128,128]{1,0:T(8,128)}, u32[]{:S(2)}) copy-start(f32[128,128]{1,0:T(8,128)} %all-reduce.4.cloned.1.call-done) | copy-start | bytes 196612
  144.4 100.6 %all-reduce.6.cloned.1.call-start = ((), (), s32[]{:S(2)}) async-start(), calls=%async_computation.8 | async-start | bytes 131072 | tf_op jit(solution)/shard_map/psum | solution.py:70
  191.0 156.3 %reduce-scatter.9.cloned.1.call-start = ((), (), s32[]{:S(2)}) async-start(), calls=%async_computation.9 | async-start | bytes 2621440 | tf_op jit(solution)/shard_map/reduce_scatter | solution.py:79
  245.0 41.2 %copy-start.5 = (f32[128,128]{1,0:T(8,128)S(1)}, f32[128,128]{1,0:T(8,128)}, u32[]{:S(2)}) copy-start(f32[128,128]{1,0:T(8,128)} %all-reduce.6.cloned.1.call-done) | copy-start | bytes 196612
  304.1 76.8 %all-gather.6.cloned.1.call-start = ((), (), s32[]{:S(2)}) async-start(), calls=%async_computation.10 | async-start | bytes 3538944 | tf_op jit(solution)/shard_map/all_gather | solution.py:82
  347.3 33.6 %copy-start.2 = (f32[96,1024]{0,1:T(8,128)S(1)}, f32[96,1024]{0,1:T(8,128)}, u32[]{:S(2)}) copy-start(f32[96,1024]{0,1:T(8,128)} %reduce-scatter.9.cloned.1.call-done) | copy-start | bytes 1179652
  349.4 72.9 %all-reduce.8.cloned.1.call-start = ((), (), s32[]{:S(2)}) async-start(), calls=%async_computation.11 | async-start | bytes 589824 | tf_op jit(solution)/shard_map/psum | solution.py:83
  386.2 244.8 %reduce-scatter.11.cloned.1.call-start = ((), (), s32[]{:S(2)}) async-start(), calls=%async_computation.12 | async-start | bytes 589824 | tf_op jit(solution)/shard_map/reduce_scatter | solution.py:93
  422.3 46.0 %copy-start.3 = (f32[96,768]{1,0:T(8,128)S(1)}, f32[96,768]{1,0:T(8,128)}, u32[]{:S(2)}) copy-start(f32[96,768]{1,0:T(8,128)} %all-reduce.8.cloned.1.call-done) | copy-start | bytes 884740
Sparse Core Ops, SparseCore 0:
  13.2 22.7 reduce-scatter.4
  47.4 31.5 all-reduce.3
  144.5 31.4 reduce-scatter.6
  191.2 53.7 all-reduce.5
  304.3 43.0 reduce-scatter.8
  349.5 31.3 all-gather.5
  386.4 35.9 all-reduce.7
  598.9 32.0 reduce-scatter.10
where the time goes:
time: 644 us; the launch traced here: 638 us
  waiting for transfers between devices  205 us (32%)
  blocking collectives  190 us (30%)
  other arithmetic  151 us (23%)
  local copies, waits for them, and re-layouts  39.1 us (6%)
  matrix products  33.9 us (5%)
  between operations  15.1 us (2%)
    psum x4, blocking collectives, on_device(): inner = lax.psum(left_product(image, image), 'row')  93.5 us
    another operation x36, other arithmetic, orthonormal(): lower = jnp.linalg.cholesky(inner)  78.2 us
    another operation x24, other arithmetic, orthonormal(): return jax.scipy.linalg.solve_triangular(lower, matrix.T, lower=True).T  66.7 us
    reduce_scatter x1, waiting for transfers between devices, on_device(): lax.psum_scatter(part_three.reshape(cells_here, rank * rank), 'col', scat...  43.1 us
    psum x1, waiting for transfers between devices, on_device(): gram_three = lax.psum(gram_part_three, 'col')  35.4 us
    all_gather x4, blocking collectives, on_device(): basis_three = lax.all_gather(own_three, 'row', axis=0, tiled=True)  35.2 us
    all_gather x1, waiting for transfers between devices, on_device(): lax.all_gather(slab_three, 'row', axis=0, tiled=True)  31.5 us
    psum x1, waiting for transfers between devices, on_device(): gram_two = lax.psum(right_product(slab_rows_two, slab_rows_two), 'row')  31 us
  transfers between devices with their start and end apart: 9, of which 7 were waited for; matrix products, arithmetic and copies ran while one was open for 15% of the time, Pallas kernels for 0%

commit v1 on v0

--- a/solution.py
+++ b/solution.py
@@ -1,14 +1,20 @@
+import functools
 import math
 
 import jax
 import jax.numpy as jnp
 from jax import lax
+from jax.experimental import pallas as pl
+from jax.experimental.pallas import tpu as pltpu
 from jax.sharding import PartitionSpec as P
 
 STEPS = 4
 
 
 HIGHEST = lax.Precision.HIGHEST
+MESH = pl.DeviceIdType.MESH
+SUBLANES = 8
+BLOCK = 8
 
 
 def product(left, right):
@@ -36,10 +42,6 @@
 def orthonormal(matrix, inner):
     lower = jnp.linalg.cholesky(inner)
     return jax.scipy.linalg.solve_triangular(lower, matrix.T, lower=True).T
-
-
-def pairing(local, block_rows):
-    return right_product(local, block_rows)
 
 
 def settle(gram_whole, basis):
@@ -49,7 +51,7 @@
     return basis
 
 
-def on_device(tensor, start_one, start_two, start_three):
+def general(tensor, start_one, start_two, start_three):
     rows_one, rows_two, depth = tensor.shape
     rank = start_three.shape[1]
     flat = tensor.reshape(rows_one * rows_two, depth)
@@ -79,7 +81,7 @@
     slab_three = lax.psum_scatter(
         part_three.reshape(cells_here, rank * rank), "col", scatter_dimension=1, tiled=True
     )
-    gram_part_three = pairing(slab_three, lax.all_gather(slab_three, "row", axis=0, tiled=True))
+    gram_part_three = right_product(slab_three, lax.all_gather(slab_three, "row", axis=0, tiled=True))
     gram_three = lax.psum(gram_part_three, "col")
     basis_three = start_three
     own_three = start_three
@@ -97,7 +99,290 @@
     return (factor_one, factor_two, factor_three, core)
 
 
+def inverse_factor(inner):
+    n = inner.shape[0]
+    groups = n // SUBLANES
+    eye = (
+        lax.broadcasted_iota(jnp.int32, (n, n), 0) == lax.broadcasted_iota(jnp.int32, (n, n), 1)
+    ).astype(jnp.float32)
+    whole = jnp.concatenate([inner, eye], axis=1)
+    width = whole.shape[1]
+    rows = [whole[g * SUBLANES : (g + 1) * SUBLANES] for g in range(groups)]
+    sub = lax.broadcasted_iota(jnp.int32, (SUBLANES, width), 0)
+    pivots = [None] * n
+    shape = (SUBLANES, width)
+    for base in range(groups):
+        columns = [
+            [jnp.broadcast_to(rows[g][:, k : k + 1], shape) for g in range(base, groups)]
+            for k in range(base * SUBLANES, (base + 1) * SUBLANES)
+        ]
+        for t in range(SUBLANES):
+            pivot = jnp.broadcast_to(columns[t][0][t : t + 1, :], shape)
+            scale = 1.0 / pivot
+            pivots[base * SUBLANES + t] = pivot
+            row = jnp.broadcast_to(rows[base][t : t + 1, :], shape)
+            heads = [
+                jnp.broadcast_to(columns[s][0][t : t + 1, :], shape) for s in range(t + 1, SUBLANES)
+            ]
+            for g in range(base, groups):
+                factor = columns[t][g - base] * scale
+                if g == base:
+                    factor = jnp.where(sub > t, factor, 0.0)
+                rows[g] = rows[g] - factor * row
+                for s in range(t + 1, SUBLANES):
+                    columns[s][g - base] = columns[s][g - base] - factor * heads[s - t - 1]
+    out = []
+    for g in range(groups):
+        held = pivots[g * SUBLANES]
+        for t in range(1, SUBLANES):
+            held = jnp.where(sub == t, pivots[g * SUBLANES + t], held)
+        out.append(rows[g] * lax.rsqrt(held))
+    return jnp.concatenate(out, axis=0)[:, n:]
+
+
+def orth(image):
+    return right_product(image, inverse_factor(left_product(image, image)))
+
+
+def steps_on(gram_ref, start_ref, basis_ref):
+    basis_ref[...] = start_ref[...]
+
+    def one(_, carry):
+        basis_ref[...] = orth(product(gram_ref[...], basis_ref[...]))
+        return carry
+
+    lax.fori_loop(0, STEPS, one, 0)
+
+
+def gram_one_kernel(held_ref, start_ref, gram_ref):
+    slabs = [product(held_ref[c], start_ref[...]) for c in range(held_ref.shape[0])]
+    total = right_product(slabs[0], slabs[0])
+    for slab in slabs[1:]:
+        total = total + right_product(slab, slab)
+    gram_ref[...] = total
+
+
+def mode_one_kernel(gram_ref, start_ref, held_ref, basis_ref, next_ref):
+    steps_on(gram_ref, start_ref, basis_ref)
+    basis = basis_ref[...]
+    total = None
+    for c in range(held_ref.shape[0]):
+        slab = left_product(held_ref[c], basis)
+        term = right_product(slab, slab)
+        total = term if total is None else total + term
+    next_ref[...] = total
+
+
+def mode_two_kernel(gram_ref, start_ref, one_ref, cube_ref, basis_ref, slab_ref):
+    steps_on(gram_ref, start_ref, basis_ref)
+    basis = basis_ref[...]
+    one = one_ref[...]
+    cells, rank, _ = slab_ref.shape
+    count = one_ref.shape[0]
+    for k in range(cells):
+        face = cube_ref[pl.ds(k, count, stride=cells), :]
+        slab_ref[k] = product(left_product(one, face), basis)
+
+
+def pack(image):
+    half = image.shape[0] // 2
+    return jnp.concatenate([image[:half], image[half:]], axis=1)
+
+
+def unpack(packed):
+    half = packed.shape[1] // 2
+    return jnp.concatenate([packed[:, :half], packed[:, half:]], axis=0)
+
+
+def apply_gram(slab, basis):
+    return pack(product(slab, left_product(slab, basis)))
+
+
+def first_image_kernel(slab_ref, basis_ref, image_ref):
+    image_ref[...] = apply_gram(slab_ref[...], basis_ref[...])
+
+
+def image_kernel(packed_ref, slab_ref, image_ref):
+    image_ref[...] = apply_gram(slab_ref[...], orth(unpack(packed_ref[...])))
+
+
+def last_kernel(packed_ref, slab_ref, factor_ref, core_ref):
+    basis = orth(unpack(packed_ref[...]))
+    factor_ref[...] = basis * math.sqrt(basis.shape[0])
+    core_ref[...] = left_product(basis, slab_ref[...])
+
+
+def on_core(kernel, shapes, *operands):
+    outs = [jax.ShapeDtypeStruct(shape, jnp.float32) for shape in shapes]
+    spec = pl.BlockSpec(memory_space=pltpu.VMEM)
+    cost = pl.CostEstimate(flops=2 * 10**9, bytes_accessed=2 * 10**6, transcendentals=0)
+    return pl.pallas_call(
+        kernel,
+        out_shape=outs,
+        in_specs=[spec] * len(operands),
+        out_specs=[spec] * len(outs),
+        cost_estimate=cost,
+    )(*operands)
+
+
+def sum_kernel(n_row, n_col, x_ref, o_ref, parts, planes, s1, r1, s2, r2, s3, r3):
+    row, col = lax.axis_index("row"), lax.axis_index("col")
+    count = x_ref.shape[0] // n_row
+
+    def mine(which):
+        return pl.ds(pl.multiple_of(which * count, SUBLANES), count)
+
+    def row_peer(d):
+        return (lax.rem(row + d, n_row), col)
+
+    def col_peer(d):
+        return (row, lax.rem(col + d, n_col))
+
+    barrier = pltpu.get_barrier_semaphore()
+    for d in range(1, n_row):
+        pl.semaphore_signal(barrier, inc=1, device_id=row_peer(d), device_id_type=MESH)
+    for d in range(1, n_col):
+        pl.semaphore_signal(barrier, inc=1, device_id=col_peer(d), device_id_type=MESH)
+    pl.semaphore_wait(barrier, n_row + n_col - 2)
+
+    def copies(n, peer, source, target, send, recv):
+        made = [
+            pltpu.make_async_remote_copy(
+                src_ref=source(d),
+                dst_ref=target(d),
+                send_sem=send.at[d],
+                recv_sem=recv.at[d],
+                device_id=peer(d),
+                device_id_type=MESH,
+            )
+            for d in range(1, n)
+        ]
+        for copy in made:
+            copy.start()
+        return made
+
+    first = copies(n_row, row_peer, lambda d: x_ref.at[mine(row_peer(d)[0])], lambda d: parts.at[d], s1, r1)
+    total = x_ref[mine(row), :]
+    for d in range(1, n_row):
+        first[d - 1].wait_recv()
+        total = total + parts[d]
+    planes[col] = total
+    second = copies(n_col, col_peer, lambda d: planes.at[col], lambda d: planes.at[col], s2, r2)
+    for copy in second:
+        copy.wait_recv()
+    total = planes[0]
+    for q in range(1, n_col):
+        total = total + planes[q]
+    o_ref[mine(row), :] = total
+    third = copies(n_row, row_peer, lambda d: o_ref.at[mine(row)], lambda d: o_ref.at[mine(row)], s3, r3)
+    for copy in third:
+        copy.wait_recv()
+    for copy in first + second + third:
+        copy.wait_send()
+
+
+def sum_all(n_row, n_col, name, collective_id, x):
+    spec = pl.BlockSpec(memory_space=pltpu.VMEM)
+    count = x.shape[0] // n_row
+    dma = pltpu.SemaphoreType.DMA
+    return pl.pallas_call(
+        functools.partial(sum_kernel, n_row, n_col),
+        out_shape=jax.ShapeDtypeStruct(x.shape, x.dtype),
+        in_specs=[spec],
+        out_specs=spec,
+        scratch_shapes=[
+            pltpu.VMEM((n_row, count, x.shape[1]), x.dtype),
+            pltpu.VMEM((n_col, count, x.shape[1]), x.dtype),
+            dma((n_row,)),
+            dma((n_row,)),
+            dma((n_col,)),
+            dma((n_col,)),
+            dma((n_row,)),
+            dma((n_row,)),
+        ],
+        compiler_params=pltpu.CompilerParams(collective_id=collective_id, has_side_effects=True),
+        cost_estimate=pl.CostEstimate(flops=10**9, bytes_accessed=10**7, transcendentals=0),
+        name=name,
+    )(x)
+
+
+def shared(n_row, n_col, tensor, start_one, start_two, start_three):
+    rows_one, rows_two, depth = tensor.shape
+    rank = start_three.shape[1]
+    both = ("row", "col")
+    n = n_row * n_col
+    n_one, n_two = rows_one * n_row, rows_two * n_col
+
+    whole_one = lax.all_gather(start_one, "row", axis=0, tiled=True)
+    whole_two = lax.all_gather(start_two, "col", axis=0, tiled=True)
+
+    flat = tensor.reshape(rows_one * rows_two, depth)
+    contracted = cross_product(start_three, flat).reshape(n, rank // n, rows_one, rows_two)
+    held = lax.all_to_all(contracted, both, split_axis=0, concat_axis=0, tiled=True)
+    held = held.reshape(n_row, n_col, rank // n, rows_one, rows_two).transpose(2, 0, 3, 1, 4)
+    held = held.reshape(rank // n, n_one, n_two)
+
+    strips = lax.all_to_all(tensor, "col", split_axis=0, concat_axis=1, tiled=True)
+    strips = strips.transpose(0, 2, 1)
+    cube = lax.all_to_all(strips, both, split_axis=1, concat_axis=0, tiled=True)
+    cells = depth // n
+    cube = cube.reshape(n_one * cells, n_two)
+
+    add = functools.partial(sum_all, n_row, n_col)
+    (part,) = on_core(gram_one_kernel, [(n_one, n_one)], held, whole_two)
+    gram_one = add("sum_gram", 1, part)
+    basis_one, part = on_core(
+        mode_one_kernel, [(n_one, rank), (n_two, n_two)], gram_one, whole_one, held
+    )
+    gram_two = add("sum_gram", 1, part)
+    basis_two, slab = on_core(
+        mode_two_kernel,
+        [(n_two, rank), (cells, rank, rank)],
+        gram_two,
+        whole_two,
+        basis_one,
+        cube,
+    )
+    own_a, own_b = rank // n_row, rank // n_col
+    slab = slab.reshape(cells, n_row, own_a, n_col, own_b).transpose(1, 3, 0, 2, 4)
+    slab = slab.reshape(n, cells, own_a * own_b)
+    slab = lax.all_to_all(slab, both, split_axis=0, concat_axis=0, tiled=True)
+    slab = slab.reshape(depth, own_a * own_b)
+
+    packed_shape = (depth // 2, 2 * rank)
+    (part,) = on_core(first_image_kernel, [packed_shape], slab, start_three)
+    for iteration in range(STEPS - 1):
+        (part,) = on_core(image_kernel, [packed_shape], add("sum_image", 2, part), slab)
+    factor_three, core = on_core(
+        last_kernel,
+        [(depth, rank), (rank, own_a * own_b)],
+        add("sum_image", 2, part),
+        slab,
+    )
+    factor_one = basis_one * math.sqrt(n_one)
+    factor_two = basis_two * math.sqrt(n_two)
+    return (factor_one, factor_two, factor_three, core.reshape(rank, own_a, own_b))
+
+
 def solution(mesh):
+    n_row, n_col = mesh.shape["row"], mesh.shape["col"]
+    n = n_row * n_col
+
+    def on_device(tensor, start_one, start_two, start_three):
+        rows_one, rows_two, depth = tensor.shape
+        rank = start_three.shape[1]
+        even = (
+            rank % n == 0
+            and depth % (2 * n_row * SUBLANES) == 0
+            and depth % (n * SUBLANES) == 0
+            and rows_one % SUBLANES == 0
+            and rows_one * n_row == rows_two * n_col
+            and rows_one % n_col == 0
+        )
+        if even:
+            return shared(n_row, n_col, tensor, start_one, start_two, start_three)
+        return general(tensor, start_one, start_two, start_three)
+
     return jax.shard_map(
         on_device,
         mesh=mesh,

time: 644 us -> 283 us (0.44)
  waiting for transfers between devices: 205 us -> 47.5 us
  other arithmetic: 151 us -> 0.96 us
  Pallas kernels: 0 us -> 148 us
  blocking collectives: 190 us -> 43.9 us
  matrix products: 33.9 us -> 4 us
  local copies, waits for them, and re-layouts: 39.1 us -> 19.9 us
  between operations: 15.1 us -> 0.82 us
  starting transfers between devices: 4.25 us -> 16.9 us
    pallas_call x0 -> x14, Pallas kernels: none -> 148 us  [the longest x6 91.6 us: sum_all(): pl.pallas_call(functools.partial(sum_kernel, n_row, n_col), out_shape=jax...]
    another operation x60 -> x0, other arithmetic: 145 us -> none  [the longest x36 78.2 us: orthonormal(): lower = jnp.linalg.cholesky(inner)]
    reduce_scatter x4 -> x0, waiting for transfers between devices: 107 us -> none  [the longest x1 43.1 us: on_device(): lax.psum_scatter(part_three.reshape(cells_here, rank * rank), 'col', scat...]
    psum x4 -> x0, blocking collectives: 93.5 us -> none  [on_device(): inner = lax.psum(left_product(image, image), 'row')]
    psum x3 -> x0, waiting for transfers between devices: 66.5 us -> none  [the longest x1 35.4 us: on_device(): gram_three = lax.psum(gram_part_three, 'col')]
    all_gather x8 -> x2, blocking collectives: 96.7 us -> 43.9 us  [the longest x1 28 us: shared(): whole_two = lax.all_gather(start_two, 'col', axis=0, tiled=True)]
    all_to_all x1 -> x4, waiting for transfers between devices: 0.01 us -> 47.5 us  [the longest x1 31.6 us: shared(): lax.all_to_all(tensor, 'col', split_axis=0, concat_axis=1, tiled=True)]
    all_gather x1 -> x0, waiting for transfers between devices: 31.5 us -> none  [on_device(): lax.all_gather(slab_three, 'row', axis=0, tiled=True)]
  transfers between devices with their start and end apart: 9 -> 4, of which waited for: 7 -> 3; matrix products, arithmetic and copies ran while one was open for 15% -> 4% of each run, Pallas kernels for 0% -> 15%
where the time goes in v1:
time: 283 us; the launch traced here: 282 us
  Pallas kernels  148 us (52%)
  waiting for transfers between devices  47.5 us (17%)
  blocking collectives  43.9 us (16%)
  local copies, waits for them, and re-layouts  19.9 us (7%)
  starting transfers between devices  16.9 us (6%)
  matrix products  4 us (1%)
    pallas_call x6, Pallas kernels, sum_all(): pl.pallas_call(functools.partial(sum_kernel, n_row, n_col), out_shape=jax...  91.6 us
    pallas_call x8, Pallas kernels, on_core(): pl.pallas_call(kernel, out_shape=outs, in_specs=[spec] * len(operands), o...  55.9 us
    all_to_all x1, waiting for transfers between devices, shared(): lax.all_to_all(tensor, 'col', split_axis=0, concat_axis=1, tiled=True)  31.6 us
    all_gather x1, blocking collectives, shared(): whole_two = lax.all_gather(start_two, 'col', axis=0, tiled=True)  28 us
    all_gather x1, blocking collectives, shared(): whole_one = lax.all_gather(start_one, 'row', axis=0, tiled=True)  15.9 us
    all_to_all x1, waiting for transfers between devices, shared(): slab = lax.all_to_all(slab, both, split_axis=0, concat_axis=0, tiled=True)  9.27 us
    all_to_all x1, waiting for transfers between devices, shared(): lax.all_to_all(contracted, both, split_axis=0, concat_axis=0, tiled=True)  6.63 us
    all_to_all x1, starting transfers between devices, shared(): lax.all_to_all(tensor, 'col', split_axis=0, concat_axis=1, tiled=True)  6.49 us
  transfers between devices with their start and end apart: 4, of which 3 were waited for; matrix products, arithmetic and copies ran while one was open for 4% of the time, Pallas kernels for 15%

profile of v1, /device:TPU:0, one launch (start us, length us, event | category | flops | bytes accessed | tf_op | source)
XLA Modules:
  0.0 281.6 jit_solution(15556553736024124312)
XLA Ops:
  0.7 6.5 %all-to-all-start.1 = ((f32[16,32,768]{2,1,0:T(8,128)}), f32[16,32,768]{2,1,0:T(8,128)S(1)}, u32[]{:S(2)}, u32[]{:S(2)}) async-start(f32[16,32,768]{2,1,0:T(8,128)} %param.4), calls=%async_computation.1 | async-start | bytes 3145728 | tf_op jit(solution)/shard_map/all_to_all | solution.py:325
  7.3 4.0 %fusion = f32[32,2,16,32]{3,0,2,1:T(8,128)S(1)} fusion(f32[16,32,768]{2,1,0:T(8,128)S(1)} %copy-done, f32[32,2,768,1]{2,1,0,3:T(2,128)S(1)} %bitcast.33), kind=kOutput, calls=%fused_computation | convolution fusion | flops 301989888 | bytes 1900544 | tf_op jit(solution)/shard_map/dot_general | solution.py:37
  12.5 31.6 %all-to-all-done.1 = f32[16,32,768]{2,1,0:T(8,128)S(1)} async-done(((f32[16,32,768]{2,1,0:T(8,128)}), f32[16,32,768]{2,1,0:T(8,128)S(1)}, u32[]{:S(2)}, u32[]{:S(2)}) %all-to-all-start.1) | async-done | bytes 1572896 | tf_op jit(solution)/shard_map/all_to_all | solution.py:325
  44.1 3.7 %all-to-all-start = ((f32[32,1,1024]{2,1,0:T(1,128)}), f32[32,1,1024]{2,1,0:T(1,128)S(1)}, u32[]{:S(2)}, u32[]{:S(2)}) async-start(f32[32,1,1024]{2,1,0:T(1,128)} %reshape.44), calls=%async_computation | async-start | bytes 262144 | tf_op jit(solution)/shard_map/all_to_all | solution.py:321
  48.0 1.6 copy.43
  49.6 6.6 %all-to-all-done = f32[32,1,1024]{2,1,0:T(1,128)S(1)} async-done(((f32[32,1,1024]{2,1,0:T(1,128)}), f32[32,1,1024]{2,1,0:T(1,128)S(1)}, u32[]{:S(2)}, u32[]{:S(2)}) %all-to-all-start) | async-done | bytes 131104 | tf_op jit(solution)/shard_map/all_to_all | solution.py:321
  56.2 2.7 all-to-all-start.2
  58.9 15.9 %all_gather.7.start_ref = f32[128,64]{1,0:T(8,128)} all-gather(f32[16,64]{1,0:T(8,128)S(1)} %copy-done.6), channel_id=1, replica_groups=mesh['row'=8,'col'=4] {'row'}, dimensions={0}, use_global_device_ids=true | all-gather | bytes 36864 | tf_op jit(solution)/shard_map/all_gather | solution.py:316
  74.8 28.0 %all_gather.6.start_ref = f32[128,64]{1,0:T(8,128)} all-gather(f32[32,64]{1,0:T(8,128)S(1)} %copy-done.5), channel_id=1, replica_groups=mesh['row'=8,'col'=4] {'col'}, dimensions={0}, use_global_device_ids=true | all-gather | bytes 40960 | tf_op jit(solution)/shard_map/all_gather | solution.py:317
  103.3 0.9 reduce
  105.7 2.2 shard_map.75.x_ref
  107.9 14.6 %sum_gram.2.gram_ref = f32[128,128]{1,0:T(8,128)} custom-call(f32[128,128]{1,0:T(8,128)} %shard_map.75.x_ref), custom_call_target="tpu_custom_call" | custom-call | flops 1000000000 | bytes 10000000 | tf_op jit(solution)/shard_map/sum_gram/pallas_call | solution.py:288
  122.5 12.5 %shard_map.76 = (f32[128,64]{1,0:T(8,128)}, f32[128,128]{1,0:T(8,128)}) custom-call(f32[128,128]{1,0:T(8,128)} %sum_gram.2.gram_ref, f32[128,64]{1,0:T(8,128)} %all_gather.7.start_ref, f32[2,128,128]{2,1,0:T(8,128)} %reshape.36.held_ref), custom_call_target="tpu_custom_call" | custom-call | flops 2000000000 | bytes 2000000 | tf_op jit(solution)/shard_map/pallas_call | solution.py:219
  135.0 13.8 %sum_gram.3.gram_ref = f32[128,128]{1,0:T(8,128)} custom-call(f32[128,128]{1,0:T(8,128)} %get-tuple-element.11.x_ref), custom_call_target="tpu_custom_call" | custom-call | flops 1000000000 | bytes 10000000 | tf_op jit(solution)/shard_map/sum_gram/pallas_call | solution.py:288
  148.9 1.4 copy.45
  150.3 15.4 %shard_map.77 = (f32[128,64]{1,0:T(8,128)}, f32[24,64,64]{2,1,0:T(8,128)}) custom-call(f32[128,128]{1,0:T(8,128)} %sum_gram.3.gram_ref, f32[128,64]{1,0:T(8,128)} %all_gather.6.start_ref, f32[128,64]{1,0:T(8,128)} %get-tuple-element.10.one_ref, f32[3072,128]{1,0:T(8,128)} %bitcast.32), custom_call_target="tpu_custom_call" | custom-call | flops 2000000000 | bytes 2000000 | tf_op jit(solution)/shard_map/pallas_call | solution.py:219
  165.7 3.1 %copy.46 = f32[24,64,64]{0,2,1:T(8,128)} copy(f32[24,64,64]{2,1,0:T(8,128)} %get-tuple-element.13) | data formatting | bytes 786432 | tf_op jit(solution)/shard_map/pallas_call | solution.py:219
  168.8 2.4 copy.47
  171.2 1.6 reshape.39
  172.8 4.0 %all-to-all-start.3 = ((f32[32,24,128]{2,1,0:T(8,128)}), f32[32,24,128]{2,1,0:T(8,128)S(1)}, u32[]{:S(2)}, u32[]{:S(2)}) async-start(f32[32,24,128]{2,1,0:T(8,128)} %reshape.39), calls=%async_computation.3 | async-start | bytes 786432 | tf_op jit(solution)/shard_map/all_to_all | solution.py:349
  179.2 9.3 %all-to-all-done.3 = f32[32,24,128]{2,1,0:T(8,128)S(1)} async-done(((f32[32,24,128]{2,1,0:T(8,128)}), f32[32,24,128]{2,1,0:T(8,128)S(1)}, u32[]{:S(2)}, u32[]{:S(2)}) %all-to-all-start.3) | async-done | bytes 393248 | tf_op jit(solution)/shard_map/all_to_all | solution.py:349
  189.2 2.8 %shard_map.78.x_ref = f32[384,128]{1,0:T(8,128)} custom-call(f32[768,128]{1,0:T(8,128)} %bitcast.35, f32[768,64]{1,0:T(8,128)} %copy.48.basis_ref), custom_call_target="tpu_custom_call" | custom-call | flops 2000000000 | bytes 2000000 | tf_op jit(solution)/shard_map/pallas_call | solution.py:219
  192.0 16.4 %sum_image.4.packed_ref = f32[384,128]{1,0:T(8,128)} custom-call(f32[384,128]{1,0:T(8,128)} %shard_map.78.x_ref), custom_call_target="tpu_custom_call" | custom-call | flops 1000000000 | bytes 10000000 | tf_op jit(solution)/shard_map/sum_image/pallas_call | solution.py:288
  208.4 6.0 %shard_map.79.x_ref = f32[384,128]{1,0:T(8,128)} custom-call(f32[384,128]{1,0:T(8,128)} %sum_image.4.packed_ref, f32[768,128]{1,0:T(8,128)} %bitcast.36), custom_call_target="tpu_custom_call" | custom-call | flops 2000000000 | bytes 2000000 | tf_op jit(solution)/shard_map/pallas_call | solution.py:219
  214.4 15.3 %sum_image.5.packed_ref = f32[384,128]{1,0:T(8,128)} custom-call(f32[384,128]{1,0:T(8,128)} %shard_map.79.x_ref), custom_call_target="tpu_custom_call" | custom-call | flops 1000000000 | bytes 10000000 | tf_op jit(solution)/shard_map/sum_image/pallas_call | solution.py:288
  229.8 6.0 %shard_map.80.x_ref = f32[384,128]{1,0:T(8,128)} custom-call(f32[384,128]{1,0:T(8,128)} %sum_image.5.packed_ref, f32[768,128]{1,0:T(8,128)} %bitcast.37), custom_call_target="tpu_custom_call" | custom-call | flops 2000000000 | bytes 2000000 | tf_op jit(solution)/shard_map/pallas_call | solution.py:219
  235.8 15.6 %sum_image.6.packed_ref = f32[384,128]{1,0:T(8,128)} custom-call(f32[384,128]{1,0:T(8,128)} %shard_map.80.x_ref), custom_call_target="tpu_custom_call" | custom-call | flops 1000000000 | bytes 10000000 | tf_op jit(solution)/shard_map/sum_image/pallas_call | solution.py:288
  251.4 6.0 %shard_map.81.x_ref = f32[384,128]{1,0:T(8,128)} custom-call(f32[384,128]{1,0:T(8,128)} %sum_image.6.packed_ref, f32[768,128]{1,0:T(8,128)} %bitcast.38), custom_call_target="tpu_custom_call" | custom-call | flops 2000000000 | bytes 2000000 | tf_op jit(solution)/shard_map/pallas_call | solution.py:219
  257.4 15.8 %sum_image.7.packed_ref = f32[384,128]{1,0:T(8,128)} custom-call(f32[384,128]{1,0:T(8,128)} %shard_map.81.x_ref), custom_call_target="tpu_custom_call" | custom-call | flops 1000000000 | bytes 10000000 | tf_op jit(solution)/shard_map/sum_image/pallas_call | solution.py:288
  273.2 5.0 %shard_map.82 = (f32[768,64]{1,0:T(8,128)}, f32[64,128]{1,0:T(8,128)}) custom-call(f32[384,128]{1,0:T(8,128)} %sum_image.7.packed_ref, f32[768,128]{1,0:T(8,128)} %bitcast.39), custom_call_target="tpu_custom_call" | custom-call | flops 2000000000 | bytes 2000000 | tf_op jit(solution)/shard_map/pallas_call | solution.py:219
  278.2 1.8 copy.52
  280.1 1.5 copy.49
  (29 shorter events, 6.6 us)
Async XLA Ops:
  0.6 6.6 %copy-start = (f32[16,32,768]{2,1,0:T(8,128)S(1)}, f32[16,32,768]{2,1,0:T(8,128)}, u32[]{:S(2)}) copy-start(f32[16,32,768]{2,1,0:T(8,128)} %param.4) | copy-start | bytes 4718596
  0.6 6.5 %copy-start.1 = (f32[768,64]{0,1:T(8,128)S(1)}, f32[768,64]{0,1:T(8,128)}, u32[]{:S(2)}) copy-start(f32[768,64]{0,1:T(8,128)} %param.7) | copy-start | bytes 589828
  0.7 43.5 %all-to-all-start.1 = ((f32[16,32,768]{2,1,0:T(8,128)}), f32[16,32,768]{2,1,0:T(8,128)S(1)}, u32[]{:S(2)}, u32[]{:S(2)}) async-start(f32[16,32,768]{2,1,0:T(8,128)} %param.4), calls=%async_computation.1 | async-start | bytes 3145728 | tf_op jit(solution)/shard_map/all_to_all | solution.py:325
  44.1 12.1 %all-to-all-start = ((f32[32,1,1024]{2,1,0:T(1,128)}), f32[32,1,1024]{2,1,0:T(1,128)S(1)}, u32[]{:S(2)}, u32[]{:S(2)}) async-start(f32[32,1,1024]{2,1,0:T(1,128)} %reshape.44), calls=%async_computation | async-start | bytes 262144 | tf_op jit(solution)/shard_map/all_to_all | solution.py:321
  49.6 9.3 %copy-start.6 = (f32[16,64]{1,0:T(8,128)S(1)}, f32[16,64]{1,0:T(8,128)}, u32[]{:S(2)}) copy-start(f32[16,64]{1,0:T(8,128)} %param.5) | copy-start | bytes 12292
  49.6 25.2 %copy-start.5 = (f32[32,64]{1,0:T(8,128)S(1)}, f32[32,64]{1,0:T(8,128)}, u32[]{:S(2)}) copy-start(f32[32,64]{1,0:T(8,128)} %param.6) | copy-start | bytes 24580
  56.2 92.6 %all-to-all-start.2 = ((f32[4,768,128]{2,0,1:T(4,128)}), f32[4,768,128]{2,0,1:T(4,128)S(1)}, u32[]{:S(2)}, u32[]{:S(2)}) async-start(f32[4,768,128]{2,0,1:T(4,128)} %copy.43), calls=%async_computation.2 | async-start | bytes 3145728 | tf_op jit(solution)/shard_map/all_to_all | solution.py:327
  171.2 6.5 %copy-start.3 = (f32[128,64]{1,0:T(8,128)S(1)}, f32[128,64]{1,0:T(8,128)}, u32[]{:S(2)}) copy-start(f32[128,64]{1,0:T(8,128)} %get-tuple-element.10.one_ref) | copy-start | bytes 98308
  172.8 5.7 %copy-start.4 = (f32[128,64]{1,0:T(8,128)S(1)}, f32[128,64]{1,0:T(8,128)}, u32[]{:S(2)}) copy-start(f32[128,64]{1,0:T(8,128)} %get-tuple-element.12) | copy-start | bytes 98308
  172.8 15.7 %all-to-all-start.3 = ((f32[32,24,128]{2,1,0:T(8,128)}), f32[32,24,128]{2,1,0:T(8,128)S(1)}, u32[]{:S(2)}, u32[]{:S(2)}) async-start(f32[32,24,128]{2,1,0:T(8,128)} %reshape.39), calls=%async_computation.3 | async-start | bytes 786432 | tf_op jit(solution)/shard_map/all_to_all | solution.py:349
  188.4 0.7 copy-start.2

commit v2 on v1

--- a/solution.py
+++ b/solution.py
@@ -14,7 +14,7 @@
 HIGHEST = lax.Precision.HIGHEST
 MESH = pl.DeviceIdType.MESH
 SUBLANES = 8
-BLOCK = 8
+LANES = 128
 
 
 def product(left, right):
@@ -173,15 +173,49 @@
     next_ref[...] = total
 
 
-def mode_two_kernel(gram_ref, start_ref, one_ref, cube_ref, basis_ref, slab_ref):
+def lane_groups(width):
+    return lax.div(lax.broadcasted_iota(jnp.int32, (1, LANES), 1), width)
+
+
+def shifted(value, amount):
+    amount = amount % LANES
+    return value if amount == 0 else pltpu.roll(value, amount, 1)
+
+
+def mode_two_kernel(n_row, n_col, gram_ref, start_ref, one_ref, cube_ref, basis_ref, send_ref, cube, mixed):
+    n, cells, span = cube_ref.shape
+    width = LANES // n_col
+    rows_one = span // width
+    group = lane_groups(width)
+    for row in range(n_row):
+        for tile in range(span // LANES):
+            blocks = [cube_ref[row * n_col + q, :, tile * LANES : (tile + 1) * LANES] for q in range(n_col)]
+            for s in range(n_col):
+                held = blocks[0]
+                held = shifted(held, -s * width)
+                for q in range(1, n_col):
+                    held = jnp.where(group == q, shifted(blocks[q], (q - s) * width), held)
+                item = row * rows_one + tile * n_col + s
+                cube[item * cells : (item + 1) * cells, :] = held
+    count, rank = one_ref.shape
+    one = one_ref[...]
+    for k in range(cells):
+        face = cube[pl.ds(k, count, stride=cells), :]
+        mixed[k * rank : (k + 1) * rank, :] = left_product(one, face)
     steps_on(gram_ref, start_ref, basis_ref)
     basis = basis_ref[...]
-    one = one_ref[...]
-    cells, rank, _ = slab_ref.shape
-    count = one_ref.shape[0]
-    for k in range(cells):
-        face = cube_ref[pl.ds(k, count, stride=cells), :]
-        slab_ref[k] = product(left_product(one, face), basis)
+    wide = jnp.concatenate([basis, jnp.zeros((basis.shape[0], LANES - rank), jnp.float32)], axis=1)
+    own_a, own_b = rank // n_row, rank // n_col
+    group = lane_groups(own_b)
+    for row in range(n_row):
+        rows = [mixed[pl.ds(row * own_a + s, cells, stride=rank), :] for s in range(own_a)]
+        slabs = product(jnp.concatenate(rows, axis=0), wide)
+        for q in range(n_col):
+            held = None
+            for s in range(own_a):
+                moved = shifted(slabs[s * cells : (s + 1) * cells], (s - q) * own_b)
+                held = moved if held is None else jnp.where(group == s, moved, held)
+            send_ref[row * n_col + q] = held
 
 
 def pack(image):
@@ -196,10 +230,6 @@
 
 def apply_gram(slab, basis):
     return pack(product(slab, left_product(slab, basis)))
-
-
-def first_image_kernel(slab_ref, basis_ref, image_ref):
-    image_ref[...] = apply_gram(slab_ref[...], basis_ref[...])
 
 
 def image_kernel(packed_ref, slab_ref, image_ref):
@@ -212,7 +242,7 @@
     core_ref[...] = left_product(basis, slab_ref[...])
 
 
-def on_core(kernel, shapes, *operands):
+def on_core(kernel, shapes, *operands, scratch=()):
     outs = [jax.ShapeDtypeStruct(shape, jnp.float32) for shape in shapes]
     spec = pl.BlockSpec(memory_space=pltpu.VMEM)
     cost = pl.CostEstimate(flops=2 * 10**9, bytes_accessed=2 * 10**6, transcendentals=0)
@@ -221,6 +251,7 @@
         out_shape=outs,
         in_specs=[spec] * len(operands),
         out_specs=[spec] * len(outs),
+        scratch_shapes=[pltpu.VMEM(shape, jnp.float32) for shape in scratch],
         cost_estimate=cost,
     )(*operands)
 
@@ -306,27 +337,162 @@
     )(x)
 
 
+def place(n_row, n_col):
+    return lax.axis_index("row") * n_col + lax.axis_index("col")
+
+
+def greet_all(n_row, n_col):
+    n = n_row * n_col
+    me = place(n_row, n_col)
+    barrier = pltpu.get_barrier_semaphore()
+
+    def one(d, carry):
+        peer = lax.rem(me + d, n)
+        pl.semaphore_signal(
+            barrier, inc=1, device_id=(peer // n_col, lax.rem(peer, n_col)), device_id_type=MESH
+        )
+        return carry
+
+    lax.fori_loop(1, n, one, 0)
+    pl.semaphore_wait(barrier, n - 1)
+
+
+def exchange_copy(n_row, n_col, d, source, target, send, recv):
+    n = n_row * n_col
+    me = place(n_row, n_col)
+    peer = lax.rem(me + d, n)
+    return pltpu.make_async_remote_copy(
+        src_ref=source.at[peer],
+        dst_ref=target.at[me],
+        send_sem=send.at[d],
+        recv_sem=recv.at[d],
+        device_id=(peer // n_col, lax.rem(peer, n_col)),
+        device_id_type=MESH,
+    )
+
+
+def start_exchange(n_row, n_col, *refs):
+    def one(d, carry):
+        exchange_copy(n_row, n_col, d, *refs).start()
+        return carry
+
+    lax.fori_loop(1, n_row * n_col, one, 0)
+
+
+def end_exchange(n_row, n_col, *refs):
+    def one(d, carry):
+        exchange_copy(n_row, n_col, d, *refs).wait()
+        return carry
+
+    lax.fori_loop(1, n_row * n_col, one, 0)
+
+
+def front_kernel(
+    n_row, n_col, flat_ref, three_ref, one_ref, two_ref,
+    held_ref, turned_ref, all_one_ref, all_two_ref,
+    parted, send, recv, s1, r1, s2, r2,
+):
+    row, col = lax.axis_index("row"), lax.axis_index("col")
+    me = place(n_row, n_col)
+    n, share, span = parted.shape
+    contracted = cross_product(three_ref[...], flat_ref[...])
+    for d in range(n):
+        parted[d] = contracted[d * share : (d + 1) * share]
+    greet_all(n_row, n_col)
+    start_exchange(n_row, n_col, parted, held_ref, send, recv)
+    count_one, count_two = one_ref.shape[0], two_ref.shape[0]
+    own_one = pl.ds(pl.multiple_of(row * count_one, SUBLANES), count_one)
+    own_two = pl.ds(pl.multiple_of(col * count_two, SUBLANES), count_two)
+    made = []
+    for d in range(1, n_row):
+        made.append(
+            pltpu.make_async_remote_copy(
+                src_ref=one_ref,
+                dst_ref=all_one_ref.at[own_one],
+                send_sem=s1.at[d],
+                recv_sem=r1.at[d],
+                device_id=(lax.rem(row + d, n_row), col),
+                device_id_type=MESH,
+            )
+        )
+    for d in range(1, n_col):
+        made.append(
+            pltpu.make_async_remote_copy(
+                src_ref=two_ref,
+                dst_ref=all_two_ref.at[own_two],
+                send_sem=s2.at[d],
+                recv_sem=r2.at[d],
+                device_id=(row, lax.rem(col + d, n_col)),
+                device_id_type=MESH,
+            )
+        )
+    for copy in made:
+        copy.start()
+    held_ref[me] = parted[me]
+    all_one_ref[own_one, :] = one_ref[...]
+    all_two_ref[own_two, :] = two_ref[...]
+    turned_ref[...] = flat_ref[...].T
+    for copy in made:
+        copy.wait()
+    end_exchange(n_row, n_col, parted, held_ref, send, recv)
+
+
+def slab_kernel(n_row, n_col, send_ref, basis_ref, slab_ref, image_ref, send, recv):
+    me = place(n_row, n_col)
+    greet_all(n_row, n_col)
+    start_exchange(n_row, n_col, send_ref, slab_ref, send, recv)
+    slab_ref[me] = send_ref[me]
+    end_exchange(n_row, n_col, send_ref, slab_ref, send, recv)
+    n, cells, width = slab_ref.shape
+    image_ref[...] = apply_gram(slab_ref[...].reshape(n * cells, width), basis_ref[...])
+
+
+def linked(kernel, n_row, n_col, collective_id, shapes, scratch, *operands):
+    outs = [jax.ShapeDtypeStruct(shape, jnp.float32) for shape in shapes]
+    spec = pl.BlockSpec(memory_space=pltpu.VMEM)
+    return pl.pallas_call(
+        functools.partial(kernel, n_row, n_col),
+        out_shape=outs,
+        in_specs=[spec] * len(operands),
+        out_specs=[spec] * len(outs),
+        scratch_shapes=scratch,
+        compiler_params=pltpu.CompilerParams(collective_id=collective_id, has_side_effects=True),
+        cost_estimate=pl.CostEstimate(flops=10**9, bytes_accessed=10**7, transcendentals=0),
+    )(*operands)
+
+
 def shared(n_row, n_col, tensor, start_one, start_two, start_three):
     rows_one, rows_two, depth = tensor.shape
     rank = start_three.shape[1]
     both = ("row", "col")
     n = n_row * n_col
     n_one, n_two = rows_one * n_row, rows_two * n_col
-
-    whole_one = lax.all_gather(start_one, "row", axis=0, tiled=True)
-    whole_two = lax.all_gather(start_two, "col", axis=0, tiled=True)
-
-    flat = tensor.reshape(rows_one * rows_two, depth)
-    contracted = cross_product(start_three, flat).reshape(n, rank // n, rows_one, rows_two)
-    held = lax.all_to_all(contracted, both, split_axis=0, concat_axis=0, tiled=True)
-    held = held.reshape(n_row, n_col, rank // n, rows_one, rows_two).transpose(2, 0, 3, 1, 4)
-    held = held.reshape(rank // n, n_one, n_two)
-
-    strips = lax.all_to_all(tensor, "col", split_axis=0, concat_axis=1, tiled=True)
-    strips = strips.transpose(0, 2, 1)
-    cube = lax.all_to_all(strips, both, split_axis=1, concat_axis=0, tiled=True)
-    cells = depth // n
-    cube = cube.reshape(n_one * cells, n_two)
+    span, share, cells = rows_one * rows_two, rank // n, depth // n
+    dma = pltpu.SemaphoreType.DMA
+
+    held, turned, whole_one, whole_two = linked(
+        front_kernel,
+        n_row,
+        n_col,
+        3,
+        [(n, share, span), (depth, span), (n_one, rank), (n_two, rank)],
+        [
+            pltpu.VMEM((n, share, span), jnp.float32),
+            dma((n,)),
+            dma((n,)),
+            dma((n_row,)),
+            dma((n_row,)),
+            dma((n_col,)),
+            dma((n_col,)),
+        ],
+        tensor.reshape(span, depth),
+        start_three,
+        start_one,
+        start_two,
+    )
+    cube = lax.all_to_all(turned.reshape(n, cells, span), both, split_axis=0, concat_axis=0, tiled=True)
+    held = held.reshape(n_row, n_col, share, rows_one, rows_two).transpose(2, 0, 3, 1, 4)
+    held = held.reshape(share, n_one, n_two)
 
     add = functools.partial(sum_all, n_row, n_col)
     (part,) = on_core(gram_one_kernel, [(n_one, n_one)], held, whole_two)
@@ -335,22 +501,28 @@
         mode_one_kernel, [(n_one, rank), (n_two, n_two)], gram_one, whole_one, held
     )
     gram_two = add("sum_gram", 1, part)
-    basis_two, slab = on_core(
-        mode_two_kernel,
-        [(n_two, rank), (cells, rank, rank)],
+    own_a, own_b = rank // n_row, rank // n_col
+    basis_two, blocks = on_core(
+        functools.partial(mode_two_kernel, n_row, n_col),
+        [(n_two, rank), (n, cells, own_a * own_b)],
         gram_two,
         whole_two,
         basis_one,
         cube,
-    )
-    own_a, own_b = rank // n_row, rank // n_col
-    slab = slab.reshape(cells, n_row, own_a, n_col, own_b).transpose(1, 3, 0, 2, 4)
-    slab = slab.reshape(n, cells, own_a * own_b)
-    slab = lax.all_to_all(slab, both, split_axis=0, concat_axis=0, tiled=True)
+        scratch=[(n_one * cells, n_two), (cells * rank, n_two)],
+    )
+    packed_shape = (depth // 2, 2 * rank)
+    slab, part = linked(
+        slab_kernel,
+        n_row,
+        n_col,
+        4,
+        [(n, cells, own_a * own_b), packed_shape],
+        [dma((n,)), dma((n,))],
+        blocks,
+        start_three,
+    )
     slab = slab.reshape(depth, own_a * own_b)
-
-    packed_shape = (depth // 2, 2 * rank)
-    (part,) = on_core(first_image_kernel, [packed_shape], slab, start_three)
     for iteration in range(STEPS - 1):
         (part,) = on_core(image_kernel, [packed_shape], add("sum_image", 2, part), slab)
     factor_three, core = on_core(
@@ -376,8 +548,8 @@
             and depth % (2 * n_row * SUBLANES) == 0
             and depth % (n * SUBLANES) == 0
             and rows_one % SUBLANES == 0
-            and rows_one * n_row == rows_two * n_col
-            and rows_one % n_col == 0
+            and rows_one * n_row == rows_two * n_col == LANES
+            and rank * rank == n * LANES
         )
         if even:
             return shared(n_row, n_col, tensor, start_one, start_two, start_three)

time: 283 us -> 219 us (0.77)
  Pallas kernels: 148 us -> 204 us
  waiting for transfers between devices: 47.5 us -> 0.01 us
  blocking collectives: 43.9 us -> 0 us
  starting transfers between devices: 16.9 us -> 3.49 us
  local copies, waits for them, and re-layouts: 19.9 us -> 9.18 us
  matrix products: 4 us -> 0 us
    all_to_all x4 -> x1, waiting for transfers between devices: 47.5 us -> 0.01 us  [shared(): lax.all_to_all(turned.reshape(n, cells, span), both, split_axis=0, concat...]
    all_gather x2 -> x0, blocking collectives: 43.9 us -> none  [the longest x1 28 us: shared(): whole_two = lax.all_gather(start_two, 'col', axis=0, tiled=True)]
    pallas_call x0 -> x2, Pallas kernels: none -> 34.5 us  [linked(): pl.pallas_call(functools.partial(kernel, n_row, n_col), out_shape=outs, i...]
    pallas_call x6, Pallas kernels: 91.6 us -> 116 us  [sum_all(): pl.pallas_call(functools.partial(sum_kernel, n_row, n_col), out_shape=jax...]
    all_to_all x4 -> x1, starting transfers between devices: 16.9 us -> 3.49 us  [shared(): lax.all_to_all(turned.reshape(n, cells, span), both, split_axis=0, concat...]
    dot_general x1 -> x0, matrix products: 4 us -> none  [cross_product(): lax.dot_general(left, right, (((0,), (1,)), ((), ())), precision=HIGHEST,...]
    transpose x2 -> x0, local copies, waits for them, and re-layouts: 3.97 us -> none  [the longest x1 2.37 us: shared(): slab.reshape(cells, n_row, own_a, n_col, own_b).transpose(1, 3, 0, 2, 4)]
    pallas_call x2 -> x1, local copies, waits for them, and re-layouts: 4.59 us -> 1.49 us  [on_core(): pl.pallas_call(kernel, out_shape=outs, in_specs=[spec] * len(operands), o...]
  transfers between devices with their start and end apart: 4 -> 1, of which waited for: 3 -> 0; matrix products, arithmetic and copies ran while one was open for 4% -> 1% of each run, Pallas kernels for 15% -> 31%
where the time goes in v2:
time: 219 us; the launch traced here: 218 us
  Pallas kernels  204 us (93%)
  local copies, waits for them, and re-layouts  9.18 us (4%)
  starting transfers between devices  3.49 us (2%)
    pallas_call x6, Pallas kernels, sum_all(): pl.pallas_call(functools.partial(sum_kernel, n_row, n_col), out_shape=jax...  116 us
    pallas_call x7, Pallas kernels, on_core(): pl.pallas_call(kernel, out_shape=outs, in_specs=[spec] * len(operands), o...  53.7 us
    pallas_call x2, Pallas kernels, linked(): pl.pallas_call(functools.partial(kernel, n_row, n_col), out_shape=outs, i...  34.5 us
    unnamed x10, local copies, waits for them, and re-layouts  6.21 us
  transfers between devices with their start and end apart: 1, of which 0 were waited for; matrix products, arithmetic and copies ran while one was open for 1% of the time, Pallas kernels for 31%

profile of v2, /device:TPU:0, one launch (start us, length us, event | category | flops | bytes accessed | tf_op | source)
XLA Modules:
  0.0 218.2 jit_solution(11096607228181236525)
XLA Ops:
  0.6 1.8 copy.15.three_ref.basis_ref
  2.5 18.1 %shard_map.75 = (f32[32,2,512]{2,1,0:T(2,128)}, f32[768,512]{1,0:T(8,128)}, f32[128,64]{1,0:T(8,128)}, f32[128,64]{1,0:T(8,128)}) custom-call(f32[512,768]{1,0:T(8,128)} %bitcast.10, f32[768,64]{1,0:T(8,128)} %copy.15.three_ref.basis_ref, f32[16,64]{1,0:T(8,128)} %one_ref.1, f32[32,64]{1,0:T(8,128)} %two_ref.1), custom_call_target="tpu_custom_call" | custom-call | flops 1000000000 | bytes 10000000 | tf_op jit(solution)/shard_map/pallas_call | solution.py:453
  20.6 0.0 copy-start.1
  20.6 3.5 %all-to-all-start = ((f32[32,24,512]{2,1,0:T(8,128)}), f32[32,24,512]{2,1,0:T(8,128)S(1)}, u32[]{:S(2)}, u32[]{:S(2)}) async-start(f32[32,24,512]{2,1,0:T(8,128)} %bitcast.8), calls=%async_computation | async-start | bytes 3145728 | tf_op jit(solution)/shard_map/all_to_all | solution.py:493
  24.1 0.0 copy-done.1
  24.1 0.2 reshape.27
  24.3 0.3 copy.23
  24.7 0.9 reshape.28.held_ref
  25.6 2.2 shard_map.76.x_ref
  27.8 39.4 %sum_gram.2.gram_ref = f32[128,128]{1,0:T(8,128)} custom-call(f32[128,128]{1,0:T(8,128)} %shard_map.76.x_ref), custom_call_target="tpu_custom_call" | custom-call | flops 1000000000 | bytes 10000000 | tf_op jit(solution)/shard_map/sum_gram/pallas_call | solution.py:319
  67.2 12.5 %shard_map.77 = (f32[128,64]{1,0:T(8,128)}, f32[128,128]{1,0:T(8,128)}) custom-call(f32[128,128]{1,0:T(8,128)} %sum_gram.2.gram_ref, f32[128,64]{1,0:T(8,128)} %get-tuple-element.18.start_ref, f32[2,128,128]{2,1,0:T(8,128)} %reshape.28.held_ref), custom_call_target="tpu_custom_call" | custom-call | flops 2000000000 | bytes 2000000 | tf_op jit(solution)/shard_map/pallas_call | solution.py:249
  79.6 0.8 broadcast_multiply_fusion.1
  80.5 0.7 copy.19
  81.2 13.7 %sum_gram.3.gram_ref = f32[128,128]{1,0:T(8,128)} custom-call(f32[128,128]{1,0:T(8,128)} %get-tuple-element.20.x_ref), custom_call_target="tpu_custom_call" | custom-call | flops 1000000000 | bytes 10000000 | tf_op jit(solution)/shard_map/sum_gram/pallas_call | solution.py:319
  94.8 0.0 all-to-all-done.cube_ref
  94.9 0.0 copy-start
  94.9 1.1 copy-done
  96.0 15.9 %shard_map.78 = (f32[128,64]{1,0:T(8,128)}, f32[32,24,128]{2,1,0:T(8,128)}) custom-call(f32[128,128]{1,0:T(8,128)} %sum_gram.3.gram_ref, f32[128,64]{1,0:T(8,128)} %get-tuple-element.17.start_ref, f32[128,64]{1,0:T(8,128)} %get-tuple-element.19.one_ref, f32[32,24,512]{2,1,0:T(8,128)} %copy-done), custom_call_target="tpu_custom_call" | custom-call | flops 2000000000 | bytes 2000000 | tf_op jit(solution)/shard_map/pallas_call | solution.py:249
  111.9 16.4 %shard_map.79 = (f32[32,24,128]{2,1,0:T(8,128)}, f32[384,128]{1,0:T(8,128)}) custom-call(f32[32,24,128]{2,1,0:T(8,128)} %get-tuple-element.23.send_ref, f32[768,64]{1,0:T(8,128)} %copy.15.three_ref.basis_ref), custom_call_target="tpu_custom_call" | custom-call | flops 1000000000 | bytes 10000000 | tf_op jit(solution)/shard_map/pallas_call | solution.py:453
  128.4 15.7 %sum_image.4.packed_ref = f32[384,128]{1,0:T(8,128)} custom-call(f32[384,128]{1,0:T(8,128)} %get-tuple-element.24.x_ref), custom_call_target="tpu_custom_call" | custom-call | flops 1000000000 | bytes 10000000 | tf_op jit(solution)/shard_map/sum_image/pallas_call | solution.py:319
  144.1 6.0 %shard_map.80.x_ref = f32[384,128]{1,0:T(8,128)} custom-call(f32[384,128]{1,0:T(8,128)} %sum_image.4.packed_ref, f32[768,128]{1,0:T(8,128)} %bitcast.11), custom_call_target="tpu_custom_call" | custom-call | flops 2000000000 | bytes 2000000 | tf_op jit(solution)/shard_map/pallas_call | solution.py:249
  150.1 15.6 %sum_image.5.packed_ref = f32[384,128]{1,0:T(8,128)} custom-call(f32[384,128]{1,0:T(8,128)} %shard_map.80.x_ref), custom_call_target="tpu_custom_call" | custom-call | flops 1000000000 | bytes 10000000 | tf_op jit(solution)/shard_map/sum_image/pallas_call | solution.py:319
  165.7 6.0 %shard_map.81.x_ref = f32[384,128]{1,0:T(8,128)} custom-call(f32[384,128]{1,0:T(8,128)} %sum_image.5.packed_ref, f32[768,128]{1,0:T(8,128)} %bitcast.12), custom_call_target="tpu_custom_call" | custom-call | flops 2000000000 | bytes 2000000 | tf_op jit(solution)/shard_map/pallas_call | solution.py:249
  171.7 15.6 %sum_image.6.packed_ref = f32[384,128]{1,0:T(8,128)} custom-call(f32[384,128]{1,0:T(8,128)} %shard_map.81.x_ref), custom_call_target="tpu_custom_call" | custom-call | flops 1000000000 | bytes 10000000 | tf_op jit(solution)/shard_map/sum_image/pallas_call | solution.py:319
  187.3 6.0 %shard_map.82.x_ref = f32[384,128]{1,0:T(8,128)} custom-call(f32[384,128]{1,0:T(8,128)} %sum_image.6.packed_ref, f32[768,128]{1,0:T(8,128)} %bitcast.13), custom_call_target="tpu_custom_call" | custom-call | flops 2000000000 | bytes 2000000 | tf_op jit(solution)/shard_map/pallas_call | solution.py:249
  193.3 15.8 %sum_image.7.packed_ref = f32[384,128]{1,0:T(8,128)} custom-call(f32[384,128]{1,0:T(8,128)} %shard_map.82.x_ref), custom_call_target="tpu_custom_call" | custom-call | flops 1000000000 | bytes 10000000 | tf_op jit(solution)/shard_map/sum_image/pallas_call | solution.py:319
  209.1 0.0 copy-start.2
  209.1 5.1 %shard_map.83 = (f32[768,64]{1,0:T(8,128)}, f32[64,128]{1,0:T(8,128)}) custom-call(f32[384,128]{1,0:T(8,128)} %sum_image.7.packed_ref, f32[768,128]{1,0:T(8,128)} %bitcast.14), custom_call_target="tpu_custom_call" | custom-call | flops 2000000000 | bytes 2000000 | tf_op jit(solution)/shard_map/pallas_call | solution.py:249
  214.2 1.8 copy.21
  216.0 1.5 copy.18
  217.5 0.0 copy-done.2
  217.5 0.7 copy.20
  (1 shorter events, 0.0 us)
Async XLA Ops:
  20.6 3.5 %copy-start.1 = (f32[32,2,512]{2,1,0:T(2,128)S(1)}, f32[32,2,512]{2,1,0:T(2,128)}, u32[]{:S(2)}) copy-start(f32[32,2,512]{2,1,0:T(2,128)} %get-tuple-element.16) | copy-start | bytes 393220
  20.6 74.3 %all-to-all-start = ((f32[32,24,512]{2,1,0:T(8,128)}), f32[32,24,512]{2,1,0:T(8,128)S(1)}, u32[]{:S(2)}, u32[]{:S(2)}) async-start(f32[32,24,512]{2,1,0:T(8,128)} %bitcast.8), calls=%async_computation | async-start | bytes 3145728 | tf_op jit(solution)/shard_map/all_to_all | solution.py:493
  94.9 1.1 copy-start
  209.1 8.4 %copy-start.2 = (f32[128,64]{1,0:T(8,128)S(1)}, f32[128,64]{1,0:T(8,128)}, u32[]{:S(2)}) copy-start(f32[128,64]{1,0:T(8,128)} %get-tuple-element.22) | copy-start | bytes 98308

commit v3 on v2

--- a/solution.py
+++ b/solution.py
@@ -162,9 +162,10 @@
     gram_ref[...] = total
 
 
-def mode_one_kernel(gram_ref, start_ref, held_ref, basis_ref, next_ref):
+def mode_one_kernel(gram_ref, start_ref, held_ref, basis_ref, factor_ref, next_ref):
     steps_on(gram_ref, start_ref, basis_ref)
     basis = basis_ref[...]
+    factor_ref[...] = (basis * math.sqrt(basis.shape[0])).T
     total = None
     for c in range(held_ref.shape[0]):
         slab = left_product(held_ref[c], basis)
@@ -182,7 +183,7 @@
     return value if amount == 0 else pltpu.roll(value, amount, 1)
 
 
-def mode_two_kernel(n_row, n_col, gram_ref, start_ref, one_ref, cube_ref, basis_ref, send_ref, cube, mixed):
+def mode_two_kernel(n_row, n_col, gram_ref, start_ref, one_ref, cube_ref, factor_ref, send_ref, basis_ref, cube, mixed):
     n, cells, span = cube_ref.shape
     width = LANES // n_col
     rows_one = span // width
@@ -204,6 +205,7 @@
         mixed[k * rank : (k + 1) * rank, :] = left_product(one, face)
     steps_on(gram_ref, start_ref, basis_ref)
     basis = basis_ref[...]
+    factor_ref[...] = (basis * math.sqrt(basis.shape[0])).T
     wide = jnp.concatenate([basis, jnp.zeros((basis.shape[0], LANES - rank), jnp.float32)], axis=1)
     own_a, own_b = rank // n_row, rank // n_col
     group = lane_groups(own_b)
@@ -228,20 +230,6 @@
     return jnp.concatenate([packed[:, :half], packed[:, half:]], axis=0)
 
 
-def apply_gram(slab, basis):
-    return pack(product(slab, left_product(slab, basis)))
-
-
-def image_kernel(packed_ref, slab_ref, image_ref):
-    image_ref[...] = apply_gram(slab_ref[...], orth(unpack(packed_ref[...])))
-
-
-def last_kernel(packed_ref, slab_ref, factor_ref, core_ref):
-    basis = orth(unpack(packed_ref[...]))
-    factor_ref[...] = basis * math.sqrt(basis.shape[0])
-    core_ref[...] = left_product(basis, slab_ref[...])
-
-
 def on_core(kernel, shapes, *operands, scratch=()):
     outs = [jax.ShapeDtypeStruct(shape, jnp.float32) for shape in shapes]
     spec = pl.BlockSpec(memory_space=pltpu.VMEM)
@@ -256,25 +244,20 @@
     )(*operands)
 
 
-def sum_kernel(n_row, n_col, x_ref, o_ref, parts, planes, s1, r1, s2, r2, s3, r3):
+def row_peer(n_row, d):
+    return (lax.rem(lax.axis_index("row") + d, n_row), lax.axis_index("col"))
+
+
+def col_peer(n_col, d):
+    return (lax.axis_index("row"), lax.rem(lax.axis_index("col") + d, n_col))
+
+
+def sum_body(n_row, n_col, x_ref, o_ref, parts, planes, s1, r1, s2, r2, s3, r3):
     row, col = lax.axis_index("row"), lax.axis_index("col")
     count = x_ref.shape[0] // n_row
 
     def mine(which):
         return pl.ds(pl.multiple_of(which * count, SUBLANES), count)
-
-    def row_peer(d):
-        return (lax.rem(row + d, n_row), col)
-
-    def col_peer(d):
-        return (row, lax.rem(col + d, n_col))
-
-    barrier = pltpu.get_barrier_semaphore()
-    for d in range(1, n_row):
-        pl.semaphore_signal(barrier, inc=1, device_id=row_peer(d), device_id_type=MESH)
-    for d in range(1, n_col):
-        pl.semaphore_signal(barrier, inc=1, device_id=col_peer(d), device_id_type=MESH)
-    pl.semaphore_wait(barrier, n_row + n_col - 2)
 
     def copies(n, peer, source, target, send, recv):
         made = [
@@ -283,7 +266,7 @@
                 dst_ref=target(d),
                 send_sem=send.at[d],
                 recv_sem=recv.at[d],
-                device_id=peer(d),
+                device_id=peer(n, d),
                 device_id_type=MESH,
             )
             for d in range(1, n)
@@ -292,7 +275,9 @@
             copy.start()
         return made
 
-    first = copies(n_row, row_peer, lambda d: x_ref.at[mine(row_peer(d)[0])], lambda d: parts.at[d], s1, r1)
+    first = copies(
+        n_row, row_peer, lambda d: x_ref.at[mine(row_peer(n_row, d)[0])], lambda d: parts.at[d], s1, r1
+    )
     total = x_ref[mine(row), :]
     for d in range(1, n_row):
         first[d - 1].wait_recv()
@@ -312,6 +297,16 @@
         copy.wait_send()
 
 
+def sum_kernel(n_row, n_col, *refs):
+    barrier = pltpu.get_barrier_semaphore()
+    for d in range(1, n_row):
+        pl.semaphore_signal(barrier, inc=1, device_id=row_peer(n_row, d), device_id_type=MESH)
+    for d in range(1, n_col):
+        pl.semaphore_signal(barrier, inc=1, device_id=col_peer(n_col, d), device_id_type=MESH)
+    pl.semaphore_wait(barrier, n_row + n_col - 2)
+    sum_body(n_row, n_col, *refs)
+
+
 def sum_all(n_row, n_col, name, collective_id, x):
     spec = pl.BlockSpec(memory_space=pltpu.VMEM)
     count = x.shape[0] // n_row
@@ -395,7 +390,7 @@
     row, col = lax.axis_index("row"), lax.axis_index("col")
     me = place(n_row, n_col)
     n, share, span = parted.shape
-    contracted = cross_product(three_ref[...], flat_ref[...])
+    contracted = right_product(three_ref[...], flat_ref[...])
     for d in range(n):
         parted[d] = contracted[d * share : (d + 1) * share]
     greet_all(n_row, n_col)
@@ -437,14 +432,45 @@
     end_exchange(n_row, n_col, parted, held_ref, send, recv)
 
 
-def slab_kernel(n_row, n_col, send_ref, basis_ref, slab_ref, image_ref, send, recv):
+def tail_kernel(
+    n_row, n_col, send_ref, start_ref, factor_ref, core_ref,
+    slab_ref, image, summed, parts, planes, send, recv, s1, r1, s2, r2, s3, r3,
+):
     me = place(n_row, n_col)
     greet_all(n_row, n_col)
     start_exchange(n_row, n_col, send_ref, slab_ref, send, recv)
     slab_ref[me] = send_ref[me]
     end_exchange(n_row, n_col, send_ref, slab_ref, send, recv)
     n, cells, width = slab_ref.shape
-    image_ref[...] = apply_gram(slab_ref[...].reshape(n * cells, width), basis_ref[...])
+
+    def slab():
+        return slab_ref[...].reshape(n * cells, width)
+
+    image[...] = pack(product(slab(), cross_product(slab(), start_ref[...])))
+
+    def one(step, carry):
+        turn = lax.rem(step, 2)
+        sum_body(
+            n_row, n_col, image, summed, parts, planes.at[turn],
+            s1, r1, s2.at[turn], r2.at[turn], s3, r3,
+        )
+        now = unpack(summed[...])
+        inverse = inverse_factor(left_product(now, now))
+
+        @pl.when(step < STEPS - 1)
+        def _():
+            basis = right_product(now, inverse)
+            image[...] = pack(product(slab(), left_product(slab(), basis)))
+
+        @pl.when(step == STEPS - 1)
+        def _():
+            turned = right_product(inverse, now)
+            factor_ref[...] = turned * math.sqrt(turned.shape[1])
+            core_ref[...] = cross_product(slab(), turned)
+
+        return carry
+
+    lax.fori_loop(0, STEPS, one, 0)
 
 
 def linked(kernel, n_row, n_col, collective_id, shapes, scratch, *operands):
@@ -486,7 +512,7 @@
             dma((n_col,)),
         ],
         tensor.reshape(span, depth),
-        start_three,
+        start_three.T,
         start_one,
         start_two,
     )
@@ -497,43 +523,47 @@
     add = functools.partial(sum_all, n_row, n_col)
     (part,) = on_core(gram_one_kernel, [(n_one, n_one)], held, whole_two)
     gram_one = add("sum_gram", 1, part)
-    basis_one, part = on_core(
-        mode_one_kernel, [(n_one, rank), (n_two, n_two)], gram_one, whole_one, held
+    basis_one, factor_one, part = on_core(
+        mode_one_kernel, [(n_one, rank), (rank, n_one), (n_two, n_two)], gram_one, whole_one, held
     )
     gram_two = add("sum_gram", 1, part)
     own_a, own_b = rank // n_row, rank // n_col
-    basis_two, blocks = on_core(
+    factor_two, blocks = on_core(
         functools.partial(mode_two_kernel, n_row, n_col),
-        [(n_two, rank), (n, cells, own_a * own_b)],
+        [(rank, n_two), (n, cells, own_a * own_b)],
         gram_two,
         whole_two,
         basis_one,
         cube,
-        scratch=[(n_one * cells, n_two), (cells * rank, n_two)],
-    )
-    packed_shape = (depth // 2, 2 * rank)
-    slab, part = linked(
-        slab_kernel,
+        scratch=[(n_two, rank), (n_one * cells, n_two), (cells * rank, n_two)],
+    )
+    packed, count = (depth // 2, 2 * rank), depth // 2 // n_row
+    factor_three, core = linked(
+        tail_kernel,
         n_row,
         n_col,
         4,
-        [(n, cells, own_a * own_b), packed_shape],
-        [dma((n,)), dma((n,))],
+        [(rank, depth), (own_a * own_b, rank)],
+        [
+            pltpu.VMEM((n, cells, own_a * own_b), jnp.float32),
+            pltpu.VMEM(packed, jnp.float32),
+            pltpu.VMEM(packed, jnp.float32),
+            pltpu.VMEM((n_row, count, 2 * rank), jnp.float32),
+            pltpu.VMEM((2, n_col, count, 2 * rank), jnp.float32),
+            dma((n,)),
+            dma((n,)),
+            dma((n_row,)),
+            dma((n_row,)),
+            dma((2, n_col)),
+            dma((2, n_col)),
+            dma((n_row,)),
+            dma((n_row,)),
+        ],
         blocks,
-        start_three,
-    )
-    slab = slab.reshape(depth, own_a * own_b)
-    for iteration in range(STEPS - 1):
-        (part,) = on_core(image_kernel, [packed_shape], add("sum_image", 2, part), slab)
-    factor_three, core = on_core(
-        last_kernel,
-        [(depth, rank), (rank, own_a * own_b)],
-        add("sum_image", 2, part),
-        slab,
-    )
-    factor_one = basis_one * math.sqrt(n_one)
-    factor_two = basis_two * math.sqrt(n_two)
-    return (factor_one, factor_two, factor_three, core.reshape(rank, own_a, own_b))
+        start_three.T,
+    )
+    factor_three = factor_three.T
+    return (factor_one.T, factor_two.T, factor_three, core.reshape(own_a, own_b, rank).transpose(2, 0, 1))
 
 
 def solution(mesh):

time: 219 us -> 193 us (0.88)
  Pallas kernels: 204 us -> 183 us
  local copies, waits for them, and re-layouts: 9.18 us -> 5.71 us
    pallas_call x2, Pallas kernels: 34.5 us -> 99.4 us  [linked(): pl.pallas_call(functools.partial(kernel, n_row, n_col), out_shape=outs, i...]
    pallas_call x6 -> x2, Pallas kernels: 116 us -> 53.1 us  [sum_all(): pl.pallas_call(functools.partial(sum_kernel, n_row, n_col), out_shape=jax...]
    pallas_call x7 -> x3, Pallas kernels: 53.7 us -> 30.6 us  [on_core(): pl.pallas_call(kernel, out_shape=outs, in_specs=[spec] * len(operands), o...]
    unnamed x10 -> x6, local copies, waits for them, and re-layouts: 6.21 us -> 4.23 us
  transfers between devices with their start and end apart: 1 -> 1, of which waited for: 0 -> 0; matrix products, arithmetic and copies ran while one was open for 1% -> 1% of each run, Pallas kernels for 31% -> 35%
where the time goes in v3:
time: 193 us
  Pallas kernels  183 us (95%)
  local copies, waits for them, and re-layouts  5.71 us (3%)
  starting transfers between devices  3.49 us (2%)
    pallas_call x2, Pallas kernels, linked(): pl.pallas_call(functools.partial(kernel, n_row, n_col), out_shape=outs, i...  99.4 us
    pallas_call x2, Pallas kernels, sum_all(): pl.pallas_call(functools.partial(sum_kernel, n_row, n_col), out_shape=jax...  53.1 us
    pallas_call x3, Pallas kernels, on_core(): pl.pallas_call(kernel, out_shape=outs, in_specs=[spec] * len(operands), o...  30.6 us
    unnamed x6, local copies, waits for them, and re-layouts  4.23 us
  transfers between devices with their start and end apart: 1, of which 0 were waited for; matrix products, arithmetic and copies ran while one was open for 1% of the time, Pallas kernels for 35%

profile of v3, /device:TPU:0, one launch (start us, length us, event | category | flops | bytes accessed | tf_op | source)
XLA Modules:
  0.0 192.9 jit_solution(11160749540751915967)
XLA Ops:
  0.6 18.1 %shard_map.75 = (f32[32,2,512]{2,1,0:T(2,128)}, f32[768,512]{1,0:T(8,128)}, f32[128,64]{1,0:T(8,128)}, f32[128,64]{1,0:T(8,128)}) custom-call(f32[512,768]{1,0:T(8,128)} %bitcast.16, f32[64,768]{1,0:T(8,128)} %bitcast.17, f32[16,64]{1,0:T(8,128)} %one_ref.1, f32[32,64]{1,0:T(8,128)} %two_ref.1), custom_call_target="tpu_custom_call" | custom-call | flops 1000000000 | bytes 10000000 | tf_op jit(solution)/shard_map/pallas_call | solution.py:479
  18.7 0.0 copy-start.1
  18.7 3.5 %all-to-all-start = ((f32[32,24,512]{2,1,0:T(8,128)}), f32[32,24,512]{2,1,0:T(8,128)S(1)}, u32[]{:S(2)}, u32[]{:S(2)}) async-start(f32[32,24,512]{2,1,0:T(8,128)} %bitcast.13), calls=%async_computation | async-start | bytes 3145728 | tf_op jit(solution)/shard_map/all_to_all | solution.py:519
  22.2 0.0 copy-done.1
  22.3 0.2 reshape.24
  22.5 0.3 copy.10
  22.8 0.9 reshape.25.held_ref
  23.8 2.2 %shard_map.76.refs_0_ = f32[128,128]{1,0:T(8,128)} custom-call(f32[2,128,128]{2,1,0:T(8,128)} %reshape.25.held_ref, f32[128,64]{1,0:T(8,128)} %get-tuple-element.16.start_ref), custom_call_target="tpu_custom_call" | custom-call | flops 2000000000 | bytes 2000000 | tf_op jit(solution)/shard_map/pallas_call | solution.py:237
  25.9 39.4 %sum_gram.2.gram_ref = f32[128,128]{1,0:T(8,128)} custom-call(f32[128,128]{1,0:T(8,128)} %shard_map.76.refs_0_), custom_call_target="tpu_custom_call" | custom-call | flops 1000000000 | bytes 10000000 | tf_op jit(solution)/shard_map/sum_gram/pallas_call | solution.py:314
  65.3 12.4 %shard_map.77 = (f32[128,64]{1,0:T(8,128)}, f32[64,128]{1,0:T(8,128)}, f32[128,128]{1,0:T(8,128)}) custom-call(f32[128,128]{1,0:T(8,128)} %sum_gram.2.gram_ref, f32[128,64]{1,0:T(8,128)} %get-tuple-element.17.start_ref, f32[2,128,128]{2,1,0:T(8,128)} %reshape.25.held_ref), custom_call_target="tpu_custom_call" | custom-call | flops 2000000000 | bytes 2000000 | tf_op jit(solution)/shard_map/pallas_call | solution.py:237
  77.8 13.7 %sum_gram.3.gram_ref = f32[128,128]{1,0:T(8,128)} custom-call(f32[128,128]{1,0:T(8,128)} %get-tuple-element.19.refs_0_), custom_call_target="tpu_custom_call" | custom-call | flops 1000000000 | bytes 10000000 | tf_op jit(solution)/shard_map/sum_gram/pallas_call | solution.py:314
  91.5 0.0 all-to-all-done.cube_ref
  91.5 0.0 copy-start
  91.5 1.1 copy-done
  92.6 16.0 %shard_map.78 = (f32[64,128]{1,0:T(8,128)}, f32[32,24,128]{2,1,0:T(8,128)}) custom-call(f32[128,128]{1,0:T(8,128)} %sum_gram.3.gram_ref, f32[128,64]{1,0:T(8,128)} %get-tuple-element.16.start_ref, f32[128,64]{1,0:T(8,128)} %get-tuple-element.20.one_ref, f32[32,24,512]{2,1,0:T(8,128)} %copy-done), custom_call_target="tpu_custom_call" | custom-call | flops 2000000000 | bytes 2000000 | tf_op jit(solution)/shard_map/pallas_call | solution.py:237
  108.6 81.3 %shard_map.79 = (f32[64,768]{1,0:T(8,128)}, f32[128,64]{1,0:T(8,128)}) custom-call(f32[32,24,128]{2,1,0:T(8,128)} %get-tuple-element.23.send_ref, f32[64,768]{1,0:T(8,128)} %bitcast.18), custom_call_target="tpu_custom_call" | custom-call | flops 1000000000 | bytes 10000000 | tf_op jit(solution)/shard_map/pallas_call | solution.py:479
  189.9 1.6 copy.13
  191.5 1.5 copy.14
Async XLA Ops:
  18.7 3.5 %copy-start.1 = (f32[32,2,512]{2,1,0:T(2,128)S(1)}, f32[32,2,512]{2,1,0:T(2,128)}, u32[]{:S(2)}) copy-start(f32[32,2,512]{2,1,0:T(2,128)} %get-tuple-element.15) | copy-start | bytes 393220
  18.7 72.7 %all-to-all-start = ((f32[32,24,512]{2,1,0:T(8,128)}), f32[32,24,512]{2,1,0:T(8,128)S(1)}, u32[]{:S(2)}, u32[]{:S(2)}) async-start(f32[32,24,512]{2,1,0:T(8,128)} %bitcast.13), calls=%async_computation | async-start | bytes 3145728 | tf_op jit(solution)/shard_map/all_to_all | solution.py:519
  91.5 1.1 copy-start
